TPU v7x, 128 devices: a whole 4x4x4 slice. The times are simulated.
128 devices in a mesh: section: 8 (over z_hi, x), tile: 16 (over z_lo, y, core).
Axes of the slice: x: 4, y: 4, z: 4 (z_hi: 2, z_lo: 2; z = z_hi * 2 + z_lo), core: 2. Of those that a mesh axis runs over, the one named last changes fastest.
Arguments:
- activations: bfloat16 [16, 16, 16, 16, 256], P('section', 'tile'), may hold values from -6 to 6
- weight: bfloat16 [8, 9, 256, 256], P('section'), may hold values from -0.125 to 0.125
- conv_bias: bfloat16 [8, 256], P('section'), may hold values from -3 to 3
- norm_gain: bfloat16 [8, 256], P('section'), may hold values from 0.099609375 to 1.8984375
- metric: bfloat16 [16, 9, 256], P('tile'), may hold values from 0.5 to 2
- neighbours: int32 [3, 16, 8], replicated, may hold values from 0 to 15, as said below
Outputs:
- advanced: bfloat16 [16, 16, 16, 16, 256], P('section', 'tile')
Inputs may be any that keep to these rules, and one draw needn't show every extreme that they name: `neighbours`: row 0 names neighbour tiles; each of the 8 columns names every tile once. Row 1 is a side or corner number 0 to 3. Row 2 is 0 or 1 for the 4 side columns and 0 for the corner columns.
All inputs are finite; a program needn't handle non-finite values.
Results may differ from a plain program's by a relative error of at most 0.0075.
Values may be sent and summed in bfloat16 or wider, within the bound.
A program may use at most 64 MiB of HBM per device.

v0:
```python
import jax
import jax.numpy as jnp
from jax import lax
from jax.sharding import PartitionSpec as P


def shifted_2(value, axis, by):
    peers = lax.axis_size(axis)
    return lax.ppermute(value, axis, [(i, (i + by) % peers) for i in range(peers)])


def normalize(states, gain_row):
    values = states.astype(jnp.float32)
    mean_sq = jnp.mean(values * values, axis=-1, keepdims=True)
    return (values * lax.rsqrt(mean_sq + 1e-05) * gain_row.astype(jnp.float32)).astype(jnp.bfloat16)


def side_strips(normed):
    side_len = normed.shape[1]
    return jnp.stack(
        [normed[:, 0], normed[:, :, side_len - 1], normed[:, side_len - 1], normed[:, :, 0]], axis=1
    )


def assemble(normed, strips, corners):
    top_row = jnp.concatenate([corners[0][:, None], strips[0], corners[1][:, None]], axis=1)
    middle = jnp.concatenate([strips[3][:, :, None], normed, strips[1][:, :, None]], axis=2)
    bottom = jnp.concatenate([corners[3][:, None], strips[2], corners[2][:, None]], axis=1)
    return jnp.concatenate([top_row[:, None], middle, bottom[:, None]], axis=1)


def convolve(padded, weight_taps, metric_taps, side_len):
    count = padded.shape[0]
    channels = padded.shape[-1]
    total = jnp.zeros((count, side_len * side_len, channels), jnp.float32)
    for row_off in range(3):
        for col_off in range(3):
            tap_index = row_off * 3 + col_off
            shifted = padded[
                :, row_off : row_off + side_len, col_off : col_off + side_len, :
            ].reshape(-1, channels)
            product = jnp.dot(shifted, weight_taps[tap_index], preferred_element_type=jnp.float32)
            product = product.reshape(count, side_len * side_len, channels)
            total = total + product * metric_taps[:, tap_index, :, None].astype(jnp.float32)
    return total


def advance(micro_batch, weight_taps, bias_row, gain_row, metric_own, own_lists):
    states = micro_batch[:, 0]
    side_len = states.shape[1]
    normed = normalize(states, gain_row)
    borders = side_strips(normed)
    gathered = lax.all_gather(borders[:, None], "tile", axis=1, tiled=True)
    strips = []
    for side_index in range(4):
        source = own_lists[0, side_index]
        which = own_lists[1, side_index]
        strip_rows = gathered[:, source, which]
        strip_rows = jnp.where(own_lists[2, side_index] == 1, strip_rows[:, ::-1], strip_rows)
        strips.append(strip_rows)
    corners = []
    for corner_index in range(4):
        source = own_lists[0, 4 + corner_index]
        which = own_lists[1, 4 + corner_index]
        rim_index = jnp.where(which < 2, 0, 2)
        position = jnp.where((which == 1) | (which == 2), side_len - 1, 0)
        corners.append(gathered[:, source, rim_index, position])
    padded = assemble(normed, strips, corners)
    conv = convolve(padded, weight_taps, metric_own, side_len)
    conv = conv.reshape(states.shape)
    result = states.astype(jnp.float32) + jax.nn.silu(conv + bias_row.astype(jnp.float32))
    return result.astype(jnp.bfloat16)[:, None]


def local(activations, weight, conv_bias, norm_gain, metric, neighbours):
    tile_id = lax.axis_index("tile")
    own_lists = lax.dynamic_index_in_dim(neighbours, tile_id, axis=1, keepdims=False)
    sections = lax.axis_size("section")
    current = activations
    for section_step in range(sections):
        current = advance(current, weight[0], conv_bias[0], norm_gain[0], metric, own_lists)
        current = shifted_2(current, "section", 1)
    return current


def solution(mesh):
    in_specs = (
        P("section", "tile", None, None, None),
        P("section", None, None, None),
        P("section", None),
        P("section", None),
        P("tile", None, None),
        P(),
    )
    out_specs = P("section", "tile", None, None, None)
    return jax.shard_map(local, mesh=mesh, in_specs=in_specs, out_specs=out_specs, check_vma=False)
```

profile of v0, /device:TPU:23, one launch (start us, length us, event | category | flops | bytes accessed | tf_op | source)
XLA Modules:
  0.0 410.0 jit_solution(11977463325912741904)
XLA Ops:
  48.6 1.2 copy-done.2
  52.1 3.6 collective-permute-start
  55.7 5.0 %collective-permute-done = bf16[2,1,16,16,256]{4,3,0,2,1:T(8,128)(2,1)S(1)} collective-permute-done((bf16[2,1,16,16,256]{4,3,0,2,1:T(8,128)(2,1)S(1)}, bf16[2,1,16,16,256]{4,3,0,2,1:T(8,128)(2,1)S(1)}, u32[]{:S(2)}, u32[]{:S(2)}) %collective-permute-start) | collective-permute-done | bytes 262176 | tf_op jit(solution)/shard_map/ppermute | solution.py:9
  62.0 34.5 %all-gather.19.cloned.1.call-done = bf16[2,64,16,256]{3,2,0,1:T(8,128)(2,1)} async-done(((bf16[2,4,16,256]{3,2,0,1:T(8,128)(2,1)}), bf16[2,64,16,256]{3,2,0,1:T(8,128)(2,1)}) %all-gather.19.cloned.1.call-update) | async-done | bytes 1048592 | tf_op jit(solution)/shard_map/all_gather | solution.py:53
  102.0 2.5 collective-permute-start.1
  104.5 5.4 %collective-permute-done.1 = bf16[2,1,16,16,256]{4,3,0,2,1:T(8,128)(2,1)S(1)} collective-permute-done((bf16[2,1,16,16,256]{4,3,0,2,1:T(8,128)(2,1)S(1)}, bf16[2,1,16,16,256]{4,3,0,2,1:T(8,128)(2,1)S(1)}, u32[]{:S(2)}, u32[]{:S(2)}) %collective-permute-start.1) | collective-permute-done | bytes 262176 | tf_op jit(solution)/shard_map/ppermute | solution.py:9
  111.2 33.9 %all-gather.21.cloned.1.call-done = bf16[2,64,16,256]{3,2,0,1:T(8,128)(2,1)} async-done(((bf16[2,4,16,256]{3,2,0,1:T(8,128)(2,1)}), bf16[2,64,16,256]{3,2,0,1:T(8,128)(2,1)}) %all-gather.21.cloned.1.call-update) | async-done | bytes 1048592 | tf_op jit(solution)/shard_map/all_gather | solution.py:53
  150.8 2.7 collective-permute-start.2
  153.4 5.4 %collective-permute-done.2 = bf16[2,1,16,16,256]{4,3,0,2,1:T(8,128)(2,1)S(1)} collective-permute-done((bf16[2,1,16,16,256]{4,3,0,2,1:T(8,128)(2,1)S(1)}, bf16[2,1,16,16,256]{4,3,0,2,1:T(8,128)(2,1)S(1)}, u32[]{:S(2)}, u32[]{:S(2)}) %collective-permute-start.2) | collective-permute-done | bytes 262176 | tf_op jit(solution)/shard_map/ppermute | solution.py:9
  160.1 33.9 %all-gather.23.cloned.1.call-done = bf16[2,64,16,256]{3,2,0,1:T(8,128)(2,1)} async-done(((bf16[2,4,16,256]{3,2,0,1:T(8,128)(2,1)}), bf16[2,64,16,256]{3,2,0,1:T(8,128)(2,1)}) %all-gather.23.cloned.1.call-update) | async-done | bytes 1048592 | tf_op jit(solution)/shard_map/all_gather | solution.py:53
  199.6 2.5 collective-permute-start.3
  202.2 5.4 %collective-permute-done.3 = bf16[2,1,16,16,256]{4,3,0,2,1:T(8,128)(2,1)S(1)} collective-permute-done((bf16[2,1,16,16,256]{4,3,0,2,1:T(8,128)(2,1)S(1)}, bf16[2,1,16,16,256]{4,3,0,2,1:T(8,128)(2,1)S(1)}, u32[]{:S(2)}, u32[]{:S(2)}) %collective-permute-start.3) | collective-permute-done | bytes 262176 | tf_op jit(solution)/shard_map/ppermute | solution.py:9
  208.9 33.9 %all-gather.25.cloned.1.call-done = bf16[2,64,16,256]{3,2,0,1:T(8,128)(2,1)} async-done(((bf16[2,4,16,256]{3,2,0,1:T(8,128)(2,1)}), bf16[2,64,16,256]{3,2,0,1:T(8,128)(2,1)}) %all-gather.25.cloned.1.call-update) | async-done | bytes 1048592 | tf_op jit(solution)/shard_map/all_gather | solution.py:53
  248.4 2.5 collective-permute-start.4
  250.9 5.4 %collective-permute-done.4 = bf16[2,1,16,16,256]{4,3,0,2,1:T(8,128)(2,1)S(1)} collective-permute-done((bf16[2,1,16,16,256]{4,3,0,2,1:T(8,128)(2,1)S(1)}, bf16[2,1,16,16,256]{4,3,0,2,1:T(8,128)(2,1)S(1)}, u32[]{:S(2)}, u32[]{:S(2)}) %collective-permute-start.4) | collective-permute-done | bytes 262176 | tf_op jit(solution)/shard_map/ppermute | solution.py:9
  257.6 33.9 %all-gather.27.cloned.1.call-done = bf16[2,64,16,256]{3,2,0,1:T(8,128)(2,1)} async-done(((bf16[2,4,16,256]{3,2,0,1:T(8,128)(2,1)}), bf16[2,64,16,256]{3,2,0,1:T(8,128)(2,1)}) %all-gather.27.cloned.1.call-update) | async-done | bytes 1048592 | tf_op jit(solution)/shard_map/all_gather | solution.py:53
  297.1 2.5 collective-permute-start.5
  299.6 5.4 %collective-permute-done.5 = bf16[2,1,16,16,256]{4,3,0,2,1:T(8,128)(2,1)S(1)} collective-permute-done((bf16[2,1,16,16,256]{4,3,0,2,1:T(8,128)(2,1)S(1)}, bf16[2,1,16,16,256]{4,3,0,2,1:T(8,128)(2,1)S(1)}, u32[]{:S(2)}, u32[]{:S(2)}) %collective-permute-start.5) | collective-permute-done | bytes 262176 | tf_op jit(solution)/shard_map/ppermute | solution.py:9
  306.5 33.7 %all-gather.29.cloned.1.call-done = bf16[2,64,16,256]{3,2,0,1:T(8,128)(2,1)} async-done(((bf16[2,4,16,256]{3,2,0,1:T(8,128)(2,1)}), bf16[2,64,16,256]{3,2,0,1:T(8,128)(2,1)}) %all-gather.29.cloned.1.call-update) | async-done | bytes 1048592 | tf_op jit(solution)/shard_map/all_gather | solution.py:53
  345.8 2.5 collective-permute-start.6
  348.3 5.4 %collective-permute-done.6 = bf16[2,1,16,16,256]{4,3,0,2,1:T(8,128)(2,1)S(1)} collective-permute-done((bf16[2,1,16,16,256]{4,3,0,2,1:T(8,128)(2,1)S(1)}, bf16[2,1,16,16,256]{4,3,0,2,1:T(8,128)(2,1)S(1)}, u32[]{:S(2)}, u32[]{:S(2)}) %collective-permute-start.6) | collective-permute-done | bytes 262176 | tf_op jit(solution)/shard_map/ppermute | solution.py:9
  355.0 34.0 %all-gather.31.cloned.1.call-done = bf16[2,64,16,256]{3,2,0,1:T(8,128)(2,1)} async-done(((bf16[2,4,16,256]{3,2,0,1:T(8,128)(2,1)}), bf16[2,64,16,256]{3,2,0,1:T(8,128)(2,1)}) %all-gather.31.cloned.1.call-update) | async-done | bytes 1048592 | tf_op jit(solution)/shard_map/all_gather | solution.py:53
  394.5 2.5 collective-permute-start.7
  397.0 5.4 %collective-permute-done.7 = bf16[2,1,16,16,256]{4,3,0,2,1:T(8,128)(2,1)S(1)} collective-permute-done((bf16[2,1,16,16,256]{4,3,0,2,1:T(8,128)(2,1)S(1)}, bf16[2,1,16,16,256]{4,3,0,2,1:T(8,128)(2,1)S(1)}, u32[]{:S(2)}, u32[]{:S(2)}) %collective-permute-start.7) | collective-permute-done | bytes 262176 | tf_op jit(solution)/shard_map/ppermute | solution.py:9
  (432 shorter events, 57.7 us)
Async XLA Ops:
  6.5 3.8 copy-start
  6.5 30.8 %copy-start.3 = (bf16[2,1,16,16,256]{4,3,2,1,0:T(8,128)(2,1)S(1)}, bf16[2,1,16,16,256]{4,3,2,1,0:T(8,128)(2,1)}, u32[]{:S(2)}) copy-start(bf16[2,1,16,16,256]{4,3,2,1,0:T(8,128)(2,1)} %param.6) | copy-start | bytes 786436
  6.5 38.8 %all-gather.17.cloned.1.call-start = ((), (), s32[]{:S(2)}) async-start(), calls=%async_computation | async-start | bytes 1114112 | tf_op jit(solution)/shard_map/all_gather | solution.py:53
  8.4 29.2 %copy-start.5 = (bf16[1,256]{1,0:T(2,128)(2,1)S(1)}, bf16[1,256]{1,0:T(2,128)(2,1)}, u32[]{:S(2)}) copy-start(bf16[1,256]{1,0:T(2,128)(2,1)} %param.8) | copy-start | bytes 1540
  8.4 36.8 %copy-start.4 = (bf16[1,9,256]{2,1,0:T(8,128)(2,1)S(1)}, bf16[1,9,256]{2,1,0:T(8,128)(2,1)}, u32[]{:S(2)}) copy-start(bf16[1,9,256]{2,1,0:T(8,128)(2,1)} %param.10) | copy-start | bytes 13828
  10.3 86.2 %all-gather.19.cloned.1.call-start = ((), (), s32[]{:S(2)}) async-start(), calls=%async_computation.1 | async-start | bytes 1114112 | tf_op jit(solution)/shard_map/all_gather | solution.py:53
  48.5 1.3 copy-start.2
  52.1 8.6 %collective-permute-start = (bf16[2,1,16,16,256]{4,3,0,2,1:T(8,128)(2,1)S(1)}, bf16[2,1,16,16,256]{4,3,0,2,1:T(8,128)(2,1)S(1)}, u32[]{:S(2)}, u32[]{:S(2)}) collective-permute-start(bf16[2,1,16,16,256]{4,3,0,2,1:T(8,128)(2,1)S(1)} %fusion.106), channel_id=1, source_target_pairs={{0,16},{16,32},{32,48},{48,64},{64,80},{80,96},{96,112},{112,0},{1... | collective-permute-start | bytes 786440 | tf_op jit(solution)/shard_map/ppermute | solution.py:9
  61.8 83.4 %all-gather.21.cloned.1.call-start = ((), (), s32[]{:S(2)}) async-start(), calls=%async_computation.2 | async-start | bytes 1114112 | tf_op jit(solution)/shard_map/all_gather | solution.py:53
  102.0 7.9 %collective-permute-start.1 = (bf16[2,1,16,16,256]{4,3,0,2,1:T(8,128)(2,1)S(1)}, bf16[2,1,16,16,256]{4,3,0,2,1:T(8,128)(2,1)S(1)}, u32[]{:S(2)}, u32[]{:S(2)}) collective-permute-start(bf16[2,1,16,16,256]{4,3,0,2,1:T(8,128)(2,1)S(1)} %fusion.109), channel_id=1, source_target_pairs={{0,16},{16,32},{32,48},{48,64},{64,80},{80,96},{96,112},{112,0},{1... | collective-permute-start | bytes 786440 | tf_op jit(solution)/shard_map/ppermute | solution.py:9
  111.0 83.0 %all-gather.23.cloned.1.call-start = ((), (), s32[]{:S(2)}) async-start(), calls=%async_computation.3 | async-start | bytes 1114112 | tf_op jit(solution)/shard_map/all_gather | solution.py:53
  150.8 8.1 %collective-permute-start.2 = (bf16[2,1,16,16,256]{4,3,0,2,1:T(8,128)(2,1)S(1)}, bf16[2,1,16,16,256]{4,3,0,2,1:T(8,128)(2,1)S(1)}, u32[]{:S(2)}, u32[]{:S(2)}) collective-permute-start(bf16[2,1,16,16,256]{4,3,0,2,1:T(8,128)(2,1)S(1)} %fusion.112), channel_id=1, source_target_pairs={{0,16},{16,32},{32,48},{48,64},{64,80},{80,96},{96,112},{112,0},{1... | collective-permute-start | bytes 786440 | tf_op jit(solution)/shard_map/ppermute | solution.py:9
  159.9 82.9 %all-gather.25.cloned.1.call-start = ((), (), s32[]{:S(2)}) async-start(), calls=%async_computation.4 | async-start | bytes 1114112 | tf_op jit(solution)/shard_map/all_gather | solution.py:53
  199.6 7.9 %collective-permute-start.3 = (bf16[2,1,16,16,256]{4,3,0,2,1:T(8,128)(2,1)S(1)}, bf16[2,1,16,16,256]{4,3,0,2,1:T(8,128)(2,1)S(1)}, u32[]{:S(2)}, u32[]{:S(2)}) collective-permute-start(bf16[2,1,16,16,256]{4,3,0,2,1:T(8,128)(2,1)S(1)} %fusion.115), channel_id=1, source_target_pairs={{0,16},{16,32},{32,48},{48,64},{64,80},{80,96},{96,112},{112,0},{1... | collective-permute-start | bytes 786440 | tf_op jit(solution)/shard_map/ppermute | solution.py:9
  208.6 82.9 %all-gather.27.cloned.1.call-start = ((), (), s32[]{:S(2)}) async-start(), calls=%async_computation.5 | async-start | bytes 1114112 | tf_op jit(solution)/shard_map/all_gather | solution.py:53
  248.4 7.9 %collective-permute-start.4 = (bf16[2,1,16,16,256]{4,3,0,2,1:T(8,128)(2,1)S(1)}, bf16[2,1,16,16,256]{4,3,0,2,1:T(8,128)(2,1)S(1)}, u32[]{:S(2)}, u32[]{:S(2)}) collective-permute-start(bf16[2,1,16,16,256]{4,3,0,2,1:T(8,128)(2,1)S(1)} %fusion.118), channel_id=1, source_target_pairs={{0,16},{16,32},{32,48},{48,64},{64,80},{80,96},{96,112},{112,0},{1... | collective-permute-start | bytes 786440 | tf_op jit(solution)/shard_map/ppermute | solution.py:9
  257.4 82.9 %all-gather.29.cloned.1.call-start = ((), (), s32[]{:S(2)}) async-start(), calls=%async_computation.6 | async-start | bytes 1114112 | tf_op jit(solution)/shard_map/all_gather | solution.py:53
  297.1 7.9 %collective-permute-start.5 = (bf16[2,1,16,16,256]{4,3,0,2,1:T(8,128)(2,1)S(1)}, bf16[2,1,16,16,256]{4,3,0,2,1:T(8,128)(2,1)S(1)}, u32[]{:S(2)}, u32[]{:S(2)}) collective-permute-start(bf16[2,1,16,16,256]{4,3,0,2,1:T(8,128)(2,1)S(1)} %fusion.121), channel_id=1, source_target_pairs={{0,16},{16,32},{32,48},{48,64},{64,80},{80,96},{96,112},{112,0},{1... | collective-permute-start | bytes 786440 | tf_op jit(solution)/shard_map/ppermute | solution.py:9
  306.1 82.9 %all-gather.31.cloned.1.call-start = ((), (), s32[]{:S(2)}) async-start(), calls=%async_computation.7 | async-start | bytes 1114112 | tf_op jit(solution)/shard_map/all_gather | solution.py:53
  345.8 7.9 %collective-permute-start.6 = (bf16[2,1,16,16,256]{4,3,0,2,1:T(8,128)(2,1)S(1)}, bf16[2,1,16,16,256]{4,3,0,2,1:T(8,128)(2,1)S(1)}, u32[]{:S(2)}, u32[]{:S(2)}) collective-permute-start(bf16[2,1,16,16,256]{4,3,0,2,1:T(8,128)(2,1)S(1)} %fusion.124), channel_id=1, source_target_pairs={{0,16},{16,32},{32,48},{48,64},{64,80},{80,96},{96,112},{112,0},{1... | collective-permute-start | bytes 786440 | tf_op jit(solution)/shard_map/ppermute | solution.py:9
  394.1 9.0 %copy-start.1 = (s32[3,16,8]{1,2,0:T(8,128)S(1)}, s32[3,16,8]{1,2,0:T(8,128)}, u32[]{:S(2)}) copy-start(s32[3,16,8]{1,2,0:T(8,128)} %param.11) | copy-start | bytes 4612
  394.5 7.9 %collective-permute-start.7 = (bf16[2,1,16,16,256]{4,3,0,2,1:T(8,128)(2,1)S(1)}, bf16[2,1,16,16,256]{4,3,0,2,1:T(8,128)(2,1)S(1)}, u32[]{:S(2)}, u32[]{:S(2)}) collective-permute-start(bf16[2,1,16,16,256]{4,3,0,2,1:T(8,128)(2,1)S(1)} %fusion.127), channel_id=1, source_target_pairs={{0,16},{16,32},{32,48},{48,64},{64,80},{80,96},{96,112},{112,0},{1... | collective-permute-start | bytes 786440 | tf_op jit(solution)/shard_map/ppermute | solution.py:9
Sparse Core Ops, SparseCore 0:
  10.4 33.8 all-gather.16
  61.9 34.5 all-gather.18
  111.1 33.9 all-gather.20
  160.0 33.9 all-gather.22
  208.8 33.9 all-gather.24
  257.5 33.9 all-gather.26
  306.2 33.9 all-gather.28
  354.9 33.9 all-gather.30
where the time goes:
time: 417 us; the launch traced here: 410 us
  waiting for transfers between devices  281 us (67%)
  between operations  49.4 us (12%)
  local copies, waits for them, and re-layouts  23.7 us (6%)
  starting transfers between devices  21.9 us (5%)
  other arithmetic  18.1 us (4%)
  matrix products  16.5 us (4%)
    all_gather x8, waiting for transfers between devices, advance(): gathered = lax.all_gather(borders[:, None], 'tile', axis=1, tiled=True)  238 us
    ppermute x8, waiting for transfers between devices, shifted_2(): lax.ppermute(value, axis, [(i, (i + by) % peers) for i in range(peers)])  42.6 us
    ppermute x8, starting transfers between devices, shifted_2(): lax.ppermute(value, axis, [(i, (i + by) % peers) for i in range(peers)])  21.4 us
    dot_general x72, matrix products, convolve(): jnp.dot(shifted, weight_taps[tap_index], preferred_element_type=jnp.float32)  16.5 us
  transfers between devices with their start and end apart: 16, of which 15 were waited for; matrix products, arithmetic and copies ran while one was open for 1% of the time, Pallas kernels for 0%

commit v1 on v0

v1 whole, which is shorter than its diff:
```python
import jax
import jax.numpy as jnp
from jax import lax
from jax.experimental import pallas as pl
from jax.experimental.pallas import tpu as pltpu
from jax.sharding import PartitionSpec as P

MESH = pl.DeviceIdType.MESH
C = 256
HALF = 9 * C // 2
F32, BF16 = jnp.float32, jnp.bfloat16
PITCH = 18


def rcopy(src, dst, send, recv, device):
    return pltpu.make_async_remote_copy(
        src_ref=src, dst_ref=dst, send_sem=send, recv_sem=recv, device_id=device, device_id_type=MESH
    )


def kernel(
    nb, act, weight, metric, bias, gain, out,
    W, V, Z, rim_a, rim_b, metr, MB, BG, bgs, PM, pad,
    act_s, act_r, met_s, met_r, w_s, w_r, bg_s, bg_r, x_s, x_r,
    rim_s, rim_r, out_s, out_r, loc, go,
):
    s, t = lax.axis_index("section"), lax.axis_index("tile")
    hi, x = s // 4, lax.rem(s, 4)
    zl, y, c = t // 8, lax.rem(t // 2, 4), lax.rem(t, 2)
    even = lax.rem(y, 2) == 0
    active = jnp.logical_and(zl == 1, even)
    relay = jnp.logical_and(zl == 1, jnp.logical_not(even))
    cross1 = jnp.logical_and(zl == 0, even)
    cross2 = jnp.logical_and(zl == 0, jnp.logical_not(even))

    def sec(h, xx):
        return h * 4 + lax.rem(xx + 8, 4)

    def tid(plane, row, core):
        return plane * 8 + 2 * lax.rem(row + 4, 4) + core

    partner = (s, t + 1 - 2 * c)
    homes = [(s, 8 + zl), (s, 12 + zl)]
    is_home = [t == 8 + zl, t == 12 + zl]

    f1_dst = [(sec(hi, x - 1), t), (sec(hi, x + 1), t)]
    f2_dst = (sec(hi, x + 2), tid(1, y - 1, c))
    e3_dst = (sec(1 - hi, x + 1), tid(1, y + 1, c))
    e0_dst = (sec(1 - hi, x), tid(1, y + 1, c))
    e1_dst = (sec(1 - hi, x - 1), tid(1, y, c))
    e2_dst = (sec(1 - hi, x + 2), tid(1, y - 1, c))
    e0_src = (sec(1 - hi, x), tid(1, y - 1, c))
    e3_src = (sec(1 - hi, x - 1), tid(1, y - 1, c))
    w_src = [
        (sec(hi, x + 1), t), (sec(hi, x - 1), t), (sec(hi, x + 2), tid(1, y + 1, c)), e0_src, e3_src,
        (sec(1 - hi, x + 1), tid(0, y, c)), (sec(1 - hi, x + 2), tid(0, y + 1, c)),
    ]

    barrier = pltpu.get_barrier_semaphore()

    def hello(device):
        pl.semaphore_signal(barrier, inc=1, device_id=device, device_id_type=MESH)

    for j in range(2):
        @pl.when(jnp.logical_not(is_home[j]))
        def _():
            hello(homes[j])

    @pl.when(active)
    def _():
        for i in range(8):
            @pl.when(t != c * 8 + i)
            def _():
                hello((s, c * 8 + i))
        for d in w_src:
            hello(d)
        hello(partner)

    @pl.when(relay)
    def _():
        for d in (f2_dst, e3_dst, e0_dst):
            hello(d)

    @pl.when(cross1)
    def _():
        hello(e1_dst)

    @pl.when(cross2)
    def _():
        hello(e2_dst)

    at_home = jnp.logical_or(is_home[0], is_home[1])
    greeted = jnp.where(at_home, 1, 2) + jnp.where(relay, 3, jnp.where(active, jnp.where(c == zl, 15, 16), 1))
    pl.semaphore_wait(barrier, greeted)

    slot = lax.rem(t, 8)
    for j in range(2):
        @pl.when(is_home[j])
        def _():
            pltpu.make_async_copy(metric.at[0], metr.at[slot], met_r.at[slot]).start()
            pltpu.make_async_copy(act.at[j], V.at[slot], act_r.at[slot]).start()

        @pl.when(jnp.logical_not(is_home[j]))
        def _():
            rcopy(metric.at[0], metr.at[slot], met_s.at[j], met_r.at[slot], homes[j]).start()
            rcopy(act.at[j], V.at[slot], act_s.at[j], act_r.at[slot], homes[j]).start()

    bgs[0:8] = jnp.broadcast_to(bias[...], (8, C))
    bgs[8:16] = jnp.broadcast_to(gain[...], (8, C))

    mine = pl.ds(pl.multiple_of(c * HALF, HALF), HALF)

    def stream(device, n):
        k = lax.rem(s - device[0] + 8, 8)
        return rcopy(weight.at[mine], W.at[k, mine], w_s.at[n], w_r.at[k], device)

    def begin(device, n):
        stream(device, n).start()

    def sent(device, n):
        stream(device, n).wait_send()

    def lines(device, n):
        k = lax.rem(s - device[0] + 8, 8)
        return rcopy(bgs, BG.at[k], bg_s.at[n], bg_r.at[k], device)

    def tell(devices):
        for n, d in enumerate(devices):
            lines(d, n).start()

    def told(devices):
        for n, d in enumerate(devices):
            lines(d, n).wait_send()

    def arrived(k):
        rcopy(weight.at[mine], W.at[k, mine], w_s.at[0], w_r.at[k], partner).wait_recv()

    @pl.when(relay)
    def _():
        tell((f2_dst, e3_dst, e0_dst))

        @pl.when(x >= 2)
        def _():
            begin(f2_dst, 0)
        pl.semaphore_wait(go, 2)
        begin(e3_dst, 1)
        sent(e3_dst, 1)
        begin(e0_dst, 2)
        sent(e0_dst, 2)

        @pl.when(x < 2)
        def _():
            begin(f2_dst, 0)
        sent(f2_dst, 0)
        told((f2_dst, e3_dst, e0_dst))

    @pl.when(cross1)
    def _():
        tell((e1_dst,))
        begin(e1_dst, 0)
        sent(e1_dst, 0)
        told((e1_dst,))

    @pl.when(cross2)
    def _():
        tell((e2_dst,))
        begin(e2_dst, 0)
        sent(e2_dst, 0)
        told((e2_dst,))

    @pl.when(active)
    def _():
        tell(f1_dst)
        for n, d in enumerate(f1_dst):
            begin(d, n)
        own_w = pltpu.make_async_copy(weight, W.at[0], loc.at[0])
        own_w.start()
        BG[0] = bgs[...]

        @pl.loop(0, 8)
        def _(i):
            g = c * 8 + i
            row = lax.broadcasted_iota(jnp.int32, (16, 128), 0)
            col = lax.broadcasted_iota(jnp.int32, (16, 128), 1)
            for side in range(4):
                flip = nb[2, g, side]
                want = side * 16 + row + flip * (15 - 2 * row)
                PM[i, side * 16:side * 16 + 16, :] = jnp.where(col == want, 1.0, 0.0).astype(BF16)
            want = jnp.zeros((16, 128), jnp.int32) - 1
            for corner in range(4):
                which = nb[1, g, 4 + corner]
                last = 15 * (((which + 1) >> 1) & 1)
                want = jnp.where(row == corner, 64 + corner * 16 + last, want)
            PM[i, 64:80, :] = jnp.where(col == want, 1.0, 0.0).astype(BF16)

        @pl.loop(0, 8)
        def _(i):
            rcopy(metric.at[0], metr.at[i], met_s.at[0], met_r.at[i], partner).wait_recv()
            for q in range(9):
                line = jnp.broadcast_to(metr[i, q:q + 1, :].astype(F32), (128, C))
                MB[i, q] = line.T.astype(BF16)

        def normed(values, k):
            mean_sq = jnp.mean(values * values, axis=-1, keepdims=True)
            return (values * lax.rsqrt(mean_sq + 1e-05) * BG[k, 8:9, :].astype(F32)).astype(BF16)

        def keep_rim(i, rim, z):
            g = c * 8 + i
            cube = z.astype(F32).reshape(16, 16, C)
            rim[4 * g] = z[0:16]
            rim[4 * g + 1] = cube[:, 15, :].astype(BF16)
            rim[4 * g + 2] = z[240:256]
            rim[4 * g + 3] = cube[:, 0, :].astype(BF16)

        def rim_copy(i, rim, par, who):
            own = pl.ds(4 * (who * 8 + i), 4)
            return rcopy(rim.at[own], rim.at[own], rim_s.at[par, i], rim_r.at[par, i], partner)

        @pl.loop(0, 8)
        def _(i):
            rcopy(act.at[0], V.at[i], act_s.at[0], act_r.at[i], partner).wait_recv()
            z = normed(V[i].astype(F32), 0)
            Z[i] = z
            keep_rim(i, rim_a, z)
            rim_copy(i, rim_a, 0, c).start()

        for d in (e0_src, e3_src):
            pl.semaphore_signal(go, inc=1, device_id=d, device_id_type=MESH)
        own_w.wait()
        for k in range(1, 8):
            rcopy(bgs, BG.at[k], bg_s.at[0], bg_r.at[k], partner).wait_recv()

        def exchange(k):
            return rcopy(W.at[k, mine], W.at[k, mine], x_s.at[k], x_r.at[k], partner)

        other = pl.ds(pl.multiple_of((1 - c) * HALF, HALF), HALF)

        def out_copy(i):
            g = c * 8 + i
            micro = y // 2
            return rcopy(V.at[i], out.at[micro], out_s.at[i], out_r.at[micro], (s, g))

        def own_copy(i):
            micro = y // 2
            return pltpu.make_async_copy(V.at[i], out.at[micro], out_r.at[micro])

        def tile_step(i, k, rim_in, rim_out, par_out):
            g = c * 8 + i
            pieces = []
            for side in range(4):
                pieces.append(rim_in[4 * nb[0, g, side] + nb[1, g, side]])
            for corner in range(4, 8):
                pieces.append(rim_in[4 * nb[0, g, corner] + (nb[1, g, corner] & 2)])
            frame = jnp.dot(PM[i], jnp.concatenate(pieces, axis=0), preferred_element_type=F32)
            z = Z[i].astype(F32)
            for h in range(2):
                lanes = slice(h * 128, h * 128 + 128)
                f, zh = frame[:, lanes], z[:, lanes]
                pad[h, 1:17, :] = f[0:16]
                pad[h, pl.ds(PITCH + 17, 16, stride=PITCH), :] = f[16:32]
                pad[h, 17 * PITCH + 1:17 * PITCH + 17, :] = f[32:48]
                pad[h, pl.ds(PITCH, 16, stride=PITCH), :] = f[48:64]
                pad[h, 0:1, :] = f[64:65]
                pad[h, 17:18, :] = f[65:66]
                pad[h, 17 * PITCH + 17:17 * PITCH + 18, :] = f[66:67]
                pad[h, 17 * PITCH:17 * PITCH + 1, :] = f[67:68]
                for r in range(16):
                    pad[h, (r + 1) * PITCH + 1:(r + 1) * PITCH + 17, :] = zh[r * 16:r * 16 + 16]
            total = None
            for b in range(3):
                shifted = [
                    jnp.concatenate(
                        [pad[h, r * PITCH + b:r * PITCH + b + 16, :].astype(BF16) for r in range(18)], axis=0
                    )
                    for h in range(2)
                ]
                for a in range(3):
                    q = 3 * a + b
                    lhs = jnp.concatenate([sh[a * 16:a * 16 + 256] * MB[i, q] for sh in shifted], axis=1)
                    part = jnp.dot(lhs, W[k, q * C:q * C + C, :], preferred_element_type=F32)
                    total = part if total is None else total + part
            half = 0.5 * (total + BG[k, 0:1, :].astype(F32))
            v = (V[i].astype(F32) + half + half * jnp.tanh(half)).astype(BF16)
            V[i] = v

            @pl.when(k < 7)
            def _():
                nz = normed(v.astype(F32), lax.rem(k + 1, 8))
                Z[i] = nz
                keep_rim(i, rim_out, nz)
                rim_copy(i, rim_out, par_out, c).start()

            @pl.when(k == 7)
            def _():
                @pl.when(t == g)
                def _():
                    own_copy(i).start()

                @pl.when(t != g)
                def _():
                    out_copy(i).start()

        def layer(k, rim_in, par_in, rim_out, par_out):
            for i in range(8):
                rim_copy(i, rim_in, par_in, 1 - c).wait_recv()

            @pl.when(k > 0)
            def _():
                rcopy(W.at[k, other], W.at[k, other], x_s.at[k], x_r.at[k], partner).wait_recv()

            @pl.loop(0, 4)
            def _(i):
                tile_step(i, k, rim_in, rim_out, par_out)

            @pl.when(k < 7)
            def _():
                arrived(k + 1)
                exchange(k + 1).start()

            @pl.loop(4, 8)
            def _(i):
                tile_step(i, k, rim_in, rim_out, par_out)

        @pl.loop(0, 4)
        def _(n):
            @pl.when(n > 0)
            def _():
                for i in range(8):
                    rim_copy(i, rim_b, 1, c).wait_send()
            layer(2 * n, rim_a, 0, rim_b, 1)
            for i in range(8):
                rim_copy(i, rim_a, 0, c).wait_send()
            layer(2 * n + 1, rim_b, 1, rim_a, 0)

        for i in range(8):
            rim_copy(i, rim_b, 1, c).wait_send()
        for k in range(1, 8):
            exchange(k).wait_send()
        for n, d in enumerate(f1_dst):
            sent(d, n)
        told(f1_dst)
        for i in range(8):
            @pl.when(t != c * 8 + i)
            def _():
                out_copy(i).wait_send()

    for j in range(2):
        @pl.when(jnp.logical_not(is_home[j]))
        def _():
            rcopy(metric.at[0], metr.at[slot], met_s.at[j], met_r.at[slot], homes[j]).wait_send()
            rcopy(act.at[j], V.at[slot], act_s.at[j], act_r.at[slot], homes[j]).wait_send()
        rcopy(V.at[0], out.at[j], out_s.at[0], out_r.at[j], partner).wait_recv()


def local(activations, weight, conv_bias, norm_gain, metric, neighbours):
    anywhere = pl.BlockSpec(memory_space=pl.ANY)
    vmem = pl.BlockSpec(memory_space=pltpu.VMEM)
    dma = pltpu.SemaphoreType.DMA
    out = pl.pallas_call(
        kernel,
        name="sphere",
        out_shape=jax.ShapeDtypeStruct((2, C, C), BF16),
        in_specs=[pl.BlockSpec(memory_space=pltpu.SMEM), anywhere, anywhere, anywhere, vmem, vmem],
        out_specs=anywhere,
        scratch_shapes=[
            pltpu.VMEM((8, 9 * C, C), BF16),
            pltpu.VMEM((8, C, C), BF16),
            pltpu.VMEM((8, C, C), BF16),
            pltpu.VMEM((64, 16, C), BF16),
            pltpu.VMEM((64, 16, C), BF16),
            pltpu.VMEM((8, 9, C), BF16),
            pltpu.VMEM((8, 9, C, 128), BF16),
            pltpu.VMEM((8, 16, C), BF16),
            pltpu.VMEM((16, C), BF16),
            pltpu.VMEM((8, 80, 128), BF16),
            pltpu.VMEM((2, 336, 128), F32),
            dma((2,)), dma((8,)), dma((2,)), dma((8,)),
            dma((3,)), dma((8,)), dma((3,)), dma((8,)),
            dma((8,)), dma((8,)),
            dma((2, 8)), dma((2, 8)), dma((8,)), dma((2,)), dma((1,)),
            pltpu.SemaphoreType.REGULAR,
        ],
        compiler_params=pltpu.CompilerParams(collective_id=0, has_side_effects=True),
    )(
        neighbours,
        activations.reshape(2, C, C),
        weight.reshape(9 * C, C),
        metric,
        conv_bias,
        norm_gain,
    )
    return out.reshape(2, 1, 16, 16, C)


def solution(mesh):
    in_specs = (
        P("section", "tile", None, None, None),
        P("section", None, None, None),
        P("section", None),
        P("section", None),
        P("tile", None, None),
        P(),
    )
    out_specs = P("section", "tile", None, None, None)
    return jax.shard_map(local, mesh=mesh, in_specs=in_specs, out_specs=out_specs, check_vma=False)
```

time: 417 us -> 107 us (0.26); the launches traced: 410 us -> 106 us
  waiting for transfers between devices: 281 us -> 0 us
  Pallas kernels: 0 us -> 103 us
  between operations: 49.4 us -> 0.01 us
  starting transfers between devices: 21.9 us -> 0 us
  local copies, waits for them, and re-layouts: 23.7 us -> 3.06 us
  other arithmetic: 18.1 us -> 0 us
  matrix products: 16.5 us -> 0 us
    all_gather x8 -> x0, waiting for transfers between devices: 238 us -> none  [advance(): gathered = lax.all_gather(borders[:, None], 'tile', axis=1, tiled=True)]
    pallas_call x0 -> x1, Pallas kernels: none -> 103 us  [local(): pl.pallas_call(kernel, name='sphere', out_shape=jax.ShapeDtypeStruct((2,...]
    ppermute x8 -> x0, waiting for transfers between devices: 42.6 us -> none  [shifted_2(): lax.ppermute(value, axis, [(i, (i + by) % peers) for i in range(peers)])]
    ppermute x8 -> x0, starting transfers between devices: 21.4 us -> none  [shifted_2(): lax.ppermute(value, axis, [(i, (i + by) % peers) for i in range(peers)])]
    dot_general x72 -> x0, matrix products: 16.5 us -> none  [convolve(): jnp.dot(shifted, weight_taps[tap_index], preferred_element_type=jnp.float32)]
    squeeze x8 -> x0, local copies, waits for them, and re-layouts: 6.33 us -> none  [advance(): strip_rows = gathered[:, source, which]]
    slice x105 -> x0, local copies, waits for them, and re-layouts: 5.79 us -> none  [the longest x80 3.87 us: convolve(): padded[:, row_off:row_off + side_len, col_off:col_off + side_len, :]]
    dynamic_slice x8 -> x0, local copies, waits for them, and re-layouts: 5.53 us -> none  [the longest x7 5.31 us: advance(): corners.append(gathered[:, source, rim_index, position])]
  transfers between devices with their start and end apart: 16 -> 0, of which waited for: 15 -> 0; matrix products, arithmetic and copies ran while one was open for 1% -> 0% of each run, Pallas kernels for 0% -> 0%
where the time goes in v1:
time: 107 us; the launch traced here: 106 us
  Pallas kernels  103 us (96%)
  local copies, waits for them, and re-layouts  3.06 us (3%)
    pallas_call x1, Pallas kernels, local(): pl.pallas_call(kernel, name='sphere', out_shape=jax.ShapeDtypeStruct((2,...  103 us
    unnamed x2, local copies, waits for them, and re-layouts  3.06 us

profile of v1, /device:TPU:23, one launch (start us, length us, event | category | flops | bytes accessed | tf_op | source)
XLA Modules:
  0.0 106.5 jit_solution(268000663291620952)
XLA Ops:
  0.0 1.4 %copy.7.nb = s32[3,16,8]{2,1,0:T(8,128)} copy(s32[3,16,8]{1,2,0:T(8,128)} %param.11) | data formatting | bytes 3072 | tf_op args[5]
  1.4 103.4 %sphere.1 = bf16[2,256,256]{2,1,0:T(8,128)(2,1)} custom-call(s32[3,16,8]{2,1,0:T(8,128)} %copy.7.nb, bf16[2,256,256]{2,1,0:T(8,128)(2,1)} %bitcast.7, bf16[2304,256]{1,0:T(8,128)(2,1)} %bitcast.5, bf16[1,9,256]{2,1,0:T(8,128)(2,1)} %metric.1, bf16[1,256]{1,0:T(2,128)(2,1)} %bias.1, bf16[1,256]{1,0:T(2,128)(2,1)} %gain.1), custom_call_target="tpu_custom_call" | custom-call | tf_op jit(solution)/shard_map/sphere/pallas_call | solution.py:359
  104.8 1.7 %copy.10 = bf16[2,1,16,16,256]{4,3,2,1,0:T(8,128)(2,1)} copy(bf16[2,1,16,16,256]{4,3,2,1,0:T(8,128)(2,1)} %bitcast.6) | data formatting | bytes 524288
